TPU v7x, 32 devices: a whole 2x2x4 slice. The times are simulated.
32 devices in a mesh: wide: 8 (over z, core), narrow: 4 (over y, x).
Axes of the slice: x: 2, y: 2, z: 4, core: 2. Of those that a mesh axis runs over, the one named last changes fastest.
Arguments:
- tokens: bfloat16 [8192, 2048], P('wide'), may hold values from -4 to 4
- cotangent: bfloat16 [8192, 2048], P('wide'), may hold values from -4 to 4
- noise_emb: float32 [128, 2048], P('wide'), may hold values from -2.5 to 2.5
- offsets: int32 [8, 16], P('wide'), may hold values from 0 to 1024, as said below
- lengths: int32 [8, 16], P('wide'), may hold values from 0 to 1024, as said below
- group_ids: int32 [8, 16], P('wide'), may hold values from 0 to 2, as said below
- group_table: float32 [3, 2048], replicated, may hold values from -2.5 to 2.5
- w_qkv: bfloat16 [3, 2048, 2048], P(None, None, 'narrow'), may hold values from -0.125 to 0.125
- w_out: bfloat16 [2048, 2048], P('narrow'), may hold values from -0.5 to 0.5
- w_up: bfloat16 [2048, 8192], P(None, 'narrow'), may hold values from -0.125 to 0.125
- b_up: float32 [8192], P('narrow'), may hold values from -2.5 to 2.5
- w_down: bfloat16 [8192, 2048], P('narrow'), may hold values from -0.09375 to 0.09375
- w_mod: bfloat16 [2048, 6, 2048], P(None, None, 'narrow'), may hold values from -0.0625 to 0.0625
- b_mod: float32 [6, 2048], P(None, 'narrow'), may hold values from -1.5 to 1.5
Outputs:
- result: bfloat16 [8192, 2048], P('wide')
- grad_tokens: bfloat16 [8192, 2048], P('wide')
- grad_noise: float32 [128, 2048], P('wide')
- grad_group_table: float32 [3, 2048], P(None, 'wide')
- grad_w_qkv: float32 [3, 2048, 2048], P(None, 'wide', 'narrow')
- grad_w_out: float32 [2048, 2048], P('narrow', 'wide')
- grad_w_up: float32 [2048, 8192], P('wide', 'narrow')
- grad_b_up: float32 [8192], P(('narrow', 'wide'))
- grad_w_down: float32 [8192, 2048], P('narrow', 'wide')
- grad_w_mod: float32 [2048, 6, 2048], P('wide', None, 'narrow')
- grad_b_mod: float32 [6, 2048], P(None, ('narrow', 'wide'))
Inputs may be any that keep to these rules, and one draw needn't show every extreme that they name: `offsets`: each index of wide holds images of one length, 1024, 256 or 64 tokens, laid end to end from token 0 and filling its 1024 tokens: slot s starts at s times that length. Slots past the last image start at 1024. Every length occurs on some index of wide. `lengths`: the length of each image slot; 0 for slots past the last image of an index of wide. `group_ids`: 0 on indices of wide with images of 1024 tokens, 1 with 256, 2 with 64, for all slots of that index; every group occurs.
All inputs are finite; a program needn't handle non-finite values.
Results may differ from a plain program's by a relative error of at most 0.018.
Values may be sent and summed in bfloat16 or wider, within the bound.
No kernel may reach another device: no remote copies, remote signals or barrier semaphores. Data moves between devices by JAX's collectives and lax.ppermute only.
A program may use at most 320 MiB of HBM per device.

v0:
```python
import jax
import jax.numpy as jnp
from jax import lax
from jax.sharding import PartitionSpec as P

HEAD_DIM = 128
highest = lax.Precision.HIGHEST


def normalize(values):
    centred = values - jnp.mean(values, axis=-1, keepdims=True)
    recip = lax.rsqrt(jnp.mean(centred * centred, axis=-1, keepdims=True) + 1e-06)
    return (centred * recip, recip)


def norm_back(grad, normed, recip):
    first = jnp.mean(grad, axis=-1, keepdims=True)
    second = jnp.mean(grad * normed, axis=-1, keepdims=True)
    return recip * (grad - first - normed * second)


def gelu_slope(values):
    cumul = 0.5 * (1.0 + lax.erf(values * 0.7071067811865476))
    density = jnp.exp(-0.5 * values * values) * 0.3989422804014327
    return cumul + values * density


def body(
    tokens,
    cotangent,
    noise_emb,
    offsets,
    lengths,
    group_ids,
    group_table,
    w_qkv,
    w_out,
    w_up,
    b_up,
    w_down,
    w_mod,
    b_mod,
):
    f32 = jnp.float32
    half = jnp.bfloat16
    tok_dev, width = tokens.shape
    slots = offsets.shape[1]
    local_width = w_qkv.shape[2]
    heads_here = local_width // HEAD_DIM
    groups = group_table.shape[0]
    positions = jnp.arange(tok_dev, dtype=jnp.int32)[:, None]
    member = ((positions >= offsets) & (positions < offsets + lengths)).astype(f32)
    image_of = jnp.dot(member, jnp.arange(slots, dtype=f32), precision=highest)
    group_hot = (group_ids[0][:, None] == jnp.arange(groups, dtype=jnp.int32)[None, :]).astype(f32)
    cond = noise_emb + jnp.dot(group_hot, group_table, precision=highest)
    silu_low = jax.nn.silu(cond).astype(half)
    mod_local = jnp.dot(
        silu_low, w_mod.reshape(width, 6 * local_width), preferred_element_type=f32
    ) + b_mod.reshape(6 * local_width)
    mod_full = lax.all_gather(
        mod_local.reshape(slots, 6, local_width), "narrow", axis=2, tiled=True
    )

    def per_token(column):
        return jnp.dot(member, mod_full[:, column], precision=highest)

    shift_a = per_token(0)
    scale_a = per_token(1)
    gate_a = per_token(2)
    shift_b = per_token(3)
    scale_b = per_token(4)
    gate_b = per_token(5)
    tok_f = tokens.astype(f32)
    normed_a, recip_a = normalize(tok_f)
    mixed_a = (normed_a * (1.0 + scale_a) + shift_a).astype(half)
    factor = HEAD_DIM ** (-0.5)
    query = (jnp.dot(mixed_a, w_qkv[0], preferred_element_type=f32) * factor).astype(half)
    keys = jnp.dot(mixed_a, w_qkv[1], preferred_element_type=f32).astype(half)
    values = jnp.dot(mixed_a, w_qkv[2], preferred_element_type=f32).astype(half)
    block_rows = min(512, tok_dev)
    blocks = tok_dev // block_rows
    q_blocks = query.reshape(blocks, block_rows, heads_here, HEAD_DIM)
    key_heads = keys.reshape(tok_dev, heads_here, HEAD_DIM)
    value_heads = values.reshape(tok_dev, heads_here, HEAD_DIM)
    image_blocks = image_of.reshape(blocks, block_rows)

    def block_scores(q_block, image_block):
        scores = jnp.einsum("qhd,khd->hqk", q_block, key_heads, preferred_element_type=f32)
        same = image_block[:, None] == image_of[None, :]
        return jnp.where(same[None], scores, -1e30)

    def forward_block(item):
        scores = block_scores(item[0], item[1])
        top = jnp.max(scores, axis=-1, keepdims=True)
        expo = jnp.exp(scores - top)
        total = jnp.sum(expo, axis=-1, keepdims=True)
        probs = expo / total
        out = jnp.einsum(
            "hqk,khd->qhd", probs.astype(half), value_heads, preferred_element_type=f32
        )
        return (out.astype(half), (top + jnp.log(total))[..., 0])

    outs, log_totals = lax.map(forward_block, (q_blocks, image_blocks))
    heads_out = outs.reshape(tok_dev, local_width)
    attended = lax.psum(jnp.dot(heads_out, w_out, preferred_element_type=f32), "narrow")
    middle = tok_f + gate_a * attended
    normed_b, recip_b = normalize(middle)
    mixed_b = (normed_b * (1.0 + scale_b) + shift_b).astype(half)
    hidden_pre = jnp.dot(mixed_b, w_up, preferred_element_type=f32) + b_up
    hidden = jax.nn.gelu(hidden_pre, approximate=False).astype(half)
    mlp_out = lax.psum(
        jnp.dot(hidden, w_down, preferred_element_type=f32).astype(jnp.bfloat16), "narrow"
    ).astype(jnp.float32)
    result = (middle + gate_b * mlp_out).astype(half)
    grad_out = cotangent.astype(f32)
    d_mlp = (grad_out * gate_b).astype(half)
    d_hidden = jnp.dot(d_mlp, w_down.T, preferred_element_type=f32).astype(half)
    d_pre = (d_hidden.astype(f32) * gelu_slope(hidden_pre)).astype(half)
    grad_b_up = jnp.sum(d_pre.astype(f32), axis=0)
    grad_w_down = jnp.dot(hidden.T, d_mlp, preferred_element_type=f32)
    grad_w_up = jnp.dot(mixed_b.T, d_pre, preferred_element_type=f32)
    d_mixed_b = lax.psum(jnp.dot(d_pre, w_up.T, preferred_element_type=f32), "narrow")
    d_middle = grad_out + norm_back(d_mixed_b * (1.0 + scale_b), normed_b, recip_b)
    d_attn = (d_middle * gate_a).astype(half)
    grad_w_out = jnp.dot(heads_out.T, d_attn, preferred_element_type=f32)
    d_heads = jnp.dot(d_attn, w_out.T, preferred_element_type=f32).astype(half)
    d_blocks = d_heads.reshape(blocks, block_rows, heads_here, HEAD_DIM)

    def backward_block(carry, item):
        grad_key, grad_value = carry
        q_block, image_block, d_block, lse_block = item
        probs = jnp.exp(block_scores(q_block, image_block) - lse_block[..., None])
        d_probs = jnp.einsum("qhd,khd->hqk", d_block, value_heads, preferred_element_type=f32)
        inner = jnp.sum(probs * d_probs, axis=-1, keepdims=True)
        d_scores = (probs * (d_probs - inner)).astype(half)
        grad_query = jnp.einsum("hqk,khd->qhd", d_scores, key_heads, preferred_element_type=f32)
        grad_key = grad_key + jnp.einsum(
            "hqk,qhd->khd", d_scores, q_block, preferred_element_type=f32
        )
        grad_value = grad_value + jnp.einsum(
            "hqk,qhd->khd", probs.astype(half), d_block, preferred_element_type=f32
        )
        return ((grad_key, grad_value), grad_query)

    zeros = jnp.zeros((tok_dev, heads_here, HEAD_DIM), f32)
    (grad_key, grad_value), grad_query = lax.scan(
        backward_block, (zeros, zeros), (q_blocks, image_blocks, d_blocks, log_totals)
    )
    d_query = (grad_query.reshape(tok_dev, local_width) * factor).astype(half)
    d_key = grad_key.reshape(tok_dev, local_width).astype(half)
    d_value = grad_value.reshape(tok_dev, local_width).astype(half)
    d_proj = jnp.stack([d_query, d_key, d_value], axis=1)
    grad_w_qkv = jnp.einsum("td,tiv->idv", mixed_a, d_proj, preferred_element_type=f32)
    d_mixed_a = lax.psum(
        jnp.einsum("tiv,idv->td", d_proj, w_qkv, preferred_element_type=f32).astype(jnp.bfloat16),
        "narrow",
    ).astype(jnp.float32)
    grad_tokens = (d_middle + norm_back(d_mixed_a * (1.0 + scale_a), normed_a, recip_a)).astype(
        half
    )
    start = lax.axis_index("narrow") * local_width

    def own(values_in):
        return lax.dynamic_slice_in_dim(values_in, start, local_width, 1)

    token_terms = jnp.stack(
        [
            own(d_mixed_a),
            own(d_mixed_a * normed_a),
            own(d_middle * attended),
            own(d_mixed_b),
            own(d_mixed_b * normed_b),
            own(grad_out * mlp_out),
        ],
        axis=1,
    )
    d_modes = jnp.einsum("ts,tcv->scv", member, token_terms, precision=highest).astype(half)
    flat_modes = d_modes.reshape(slots, 6 * local_width)
    d_silu = lax.psum(
        jnp.dot(
            flat_modes, w_mod.reshape(width, 6 * local_width).T, preferred_element_type=f32
        ).astype(jnp.bfloat16),
        "narrow",
    ).astype(jnp.float32)
    sigma = jax.nn.sigmoid(cond)
    grad_noise = d_silu * sigma * (1.0 + cond * (1.0 - sigma))
    grad_table = jnp.dot(group_hot.T, grad_noise, precision=highest)
    grad_b_mod = jnp.sum(d_modes.astype(f32), axis=0)
    grad_w_mod = jnp.dot(silu_low.T, flat_modes, preferred_element_type=f32).reshape(
        width, 6, local_width
    )
    summed = (
        lax.psum_scatter(
            grad_w_qkv.astype(jnp.bfloat16), "wide", scatter_dimension=1, tiled=True
        ).astype(jnp.float32),
        lax.psum_scatter(
            grad_w_out.astype(jnp.bfloat16), "wide", scatter_dimension=1, tiled=True
        ).astype(jnp.float32),
        lax.psum_scatter(
            grad_w_up.astype(jnp.bfloat16), "wide", scatter_dimension=0, tiled=True
        ).astype(jnp.float32),
        lax.psum_scatter(
            grad_b_up.astype(jnp.bfloat16), "wide", scatter_dimension=0, tiled=True
        ).astype(jnp.float32),
        lax.psum_scatter(
            grad_w_down.astype(jnp.bfloat16), "wide", scatter_dimension=1, tiled=True
        ).astype(jnp.float32),
        lax.psum_scatter(
            grad_w_mod.astype(jnp.bfloat16), "wide", scatter_dimension=0, tiled=True
        ).astype(jnp.float32),
        lax.psum_scatter(
            grad_b_mod.astype(jnp.bfloat16), "wide", scatter_dimension=1, tiled=True
        ).astype(jnp.float32),
        lax.psum_scatter(
            grad_table.astype(jnp.bfloat16), "wide", scatter_dimension=1, tiled=True
        ).astype(jnp.float32),
    )
    return (
        result,
        grad_tokens,
        grad_noise,
        summed[7],
        summed[0],
        summed[1],
        summed[2],
        summed[3],
        summed[4],
        summed[5],
        summed[6],
    )


def solution(mesh):
    in_specs = (
        P("wide", None),
        P("wide", None),
        P("wide", None),
        P("wide", None),
        P("wide", None),
        P("wide", None),
        P(),
        P(None, None, "narrow"),
        P("narrow", None),
        P(None, "narrow"),
        P("narrow"),
        P("narrow", None),
        P(None, None, "narrow"),
        P(None, "narrow"),
    )
    out_specs = (
        P("wide", None),
        P("wide", None),
        P("wide", None),
        P(None, "wide"),
        P(None, "wide", "narrow"),
        P("narrow", "wide"),
        P("wide", "narrow"),
        P(("narrow", "wide")),
        P("narrow", "wide"),
        P("wide", None, "narrow"),
        P(None, ("narrow", "wide")),
    )
    return jax.shard_map(body, mesh=mesh, in_specs=in_specs, out_specs=out_specs, check_vma=False)
```

profile of v0, /device:TPU:0, one launch (start us, length us, event | category | flops | bytes accessed | tf_op | source)
XLA Modules:
  0.0 1386.5 jit_solution(8295451466740319210)
XLA Ops:
  13.7 17.1 %copy.59 = bf16[2048,6,512]{0,2,1:T(8,128)(2,1)} copy(bf16[2048,6,512]{2,0,1:T(8,128)(2,1)} %param.30) | data formatting | bytes 25165824 | tf_op args[12]
  39.8 15.2 %all_gather.3 = f32[16,6,2048]{2,1,0:T(8,128)S(1)} all-gather(f32[16,6,512]{2,1,0:T(8,128)S(1)} %reshape.223), channel_id=1, replica_groups=mesh['wide'=8,'narrow'=4] {'narrow'}, dimensions={2}, use_global_device_ids=true | all-gather | bytes 983040 | tf_op jit(solution)/shard_map/all_gather | solution.py:60
  83.1 19.1 %while.27 = (s32[]{:T(128)}, bf16[2,512,4,128]{3,2,1,0:T(4,128)(2,1)}, f32[2,4,512]{2,1,0:T(4,128)}, f32[2,512]{1,0:T(2,128)S(1)}, f32[1024]{0:T(1024)S(1)}, /*i...) while((s32[]{:T(128)}, ...), condition=%wide.region_5.6_spmd, body=%wide.region_2.5_spmd.sunk | while | flops 1093400576 | bytes 44247296 | solution.py:103
  122.5 159.6 %all-reduce.7.cloned.1.call-done = f32[1024,2048]{1,0:T(8,128)} async-done(((f32[1024,2048]{1,0:T(8,128)}), f32[1024,2048]{1,0:T(8,128)}) %all-reduce.7.cloned.1.call-update) | async-done | bytes 8388624 | tf_op jit(solution)/shard_map/psum | solution.py:105
  308.1 31.0 %fusion.32 = (bf16[1024,2048]{1,0:T(8,128)(2,1)}, f32[1024,2048]{1,0:T(8,128)}) fusion(f32[2048]{0:T(1024)S(1)} %copy-done.53, bf16[1024,2048]{1,0:T(8,128)(2,1)S(1)} %add_convert_fusion.2, bf16[2048,2048]{1,0:T(8,128)(2,1)} %param.27), kind=kOutput, calls=%fused_computation.52 | convolution fusion | flops 8728346624 | bytes 25174016 | tf_op jit(solution)/shard_map/dot_general | solution.py:109
  339.1 20.5 %fusion.117 = (bf16[2048]{0:T(1024)(128)(2,1)}, bf16[1024,2048]{1,0:T(8,128)(2,1)}) fusion(f32[1024,2048]{1,0:T(8,128)} %get-tuple-element.305, f32[2048]{0:T(1024)S(1)} %copy-done.53, bf16[2048,2048]{1,0:T(8,128)(2,1)} %param.29, f32[1024,2048]{1,0:T(8,128)} %fusion.84, bf16[1024,2048]{1,0:T(8,128)(2,1)} %param.19), kind=kOutput, calls=%fused_computation.182 | convolution fusion | flops 8625584128 | bytes 33566720 | tf_op jit(solution)/shard_map/dot_general | solution.py:117
  359.6 14.7 %fusion.119 = f32[1024,2048]{1,0:T(8,128)} fusion(bf16[1024,2048]{1,0:T(8,128)(2,1)} %get-tuple-element.307, bf16[2048,2048]{1,0:T(8,128)(2,1)} %param.27), kind=kOutput, calls=%fused_computation.185 | convolution fusion | flops 8589934592 | bytes 20971520 | tf_op jit(solution)/shard_map/dot_general | solution.py:122
  374.4 13.8 convolution_convert_fusion.3
  388.2 159.1 %all-reduce.9.cloned.1.call-done = f32[1024,2048]{1,0:T(8,128)} async-done(((f32[1024,2048]{1,0:T(8,128)}), f32[1024,2048]{1,0:T(8,128)}) %all-reduce.9.cloned.1.call-update) | async-done | bytes 8388624 | tf_op jit(solution)/shard_map/psum | solution.py:122
  556.7 18.6 %multiply_convert_fusion.1 = (bf16[1024,2048]{1,0:T(8,128)(2,1)}, f32[1024,2048]{1,0:T(8,128)}) fusion(f32[1024,2048]{1,0:T(8,128)} %get-tuple-element.303, f32[1024]{0:T(1024)S(1)} %get-tuple-element.310, f32[1024]{0:T(1024)S(1)} %get-tuple-element.311, f32[1024,2048]{1,0:T(8,128)} %all-reduce.9.cloned.1.call-done, f32[1024,2048]{1,0:T(8,128)} %fusion.81, ...), kind=kLoop, calls=%fused_computation.62 | loop fusion | flops 25165824 | bytes 50348032 | tf_op jit(solution)/shard_map/convert_element_type | solution.py:124
  583.2 33.3 %while.28 = (s32[]{:T(128)}, f32[1024,4,128]{0,2,1:T(8,128)}, f32[1024,4,128]{0,2,1:T(8,128)}, f32[2,512,4,128]{3,1,2,0:T(8,128)}, bf16[2,512,4,128]{3,1,2,0:T(8...) while((s32[]{:T(128)}, f32[1024,4,128]{0,2,1:T(8,128)}, ...), condition=%wide.region_15.16_spmd.clone, body=%wide.region_13.15_spmd.clone.sunk | while | flops 2712139776 | bytes 139528592 | solution.py:146
  624.0 10.9 bitcast_convert_fusion
  641.8 166.5 %all-reduce.13.cloned.1.call-done = (bf16[1024,2048]{1,0:T(8,128)(2,1)}, bf16[1024,2048]{1,0:T(8,128)(2,1)}) async-done(((bf16[1024,2048]{1,0:T(8,128)(2,1)}, bf16[1024,2048]{1,0:T(8,128)(2,1)}), (bf16[1024,2048]{1,0:T(8,128)(2,1)}, bf16[1024,2048]{1,0:T(8,128)(2,1)})) %all-reduce.13.cloned.1.call-update) | async-done | bytes 8388624 | tf_op jit(solution)/shard_map/psum | solution.py:111
  857.5 14.3 %convolution_convert_fusion.1 = bf16[2048,2048]{1,0:T(8,128)(2,1)} fusion(bf16[1024,2048]{1,0:T(8,128)(2,1)} %copy-done.19, bf16[1024,2048]{1,0:T(8,128)(2,1)} %get-tuple-element.307), kind=kOutput, calls=%fused_computation.89 | convolution fusion | flops 8594128896 | bytes 16777216 | tf_op jit(solution)/shard_map/dot_general | solution.py:121
  871.9 15.3 %convolution_convert_fusion = bf16[2048,2048]{1,0:T(8,128)(2,1)} fusion(bf16[1024,2048]{1,0:T(8,128)(2,1)} %get-tuple-element.304, f32[1024,2048]{1,0:T(8,128)} %fusion.84, bf16[1024,2048]{1,0:T(8,128)(2,1)} %param.19), kind=kOutput, calls=%fused_computation.88 | convolution fusion | flops 8600420352 | bytes 25165824 | tf_op jit(solution)/shard_map/dot_general | solution.py:120
  896.2 11.3 convert_bitcast_fusion
  916.0 16.1 %all-reduce = bf16[2048]{0:T(1024)(128)(2,1)S(1)} all-reduce(bf16[2048]{0:T(1024)(128)(2,1)S(1)} %copy-done.47), channel_id=6, replica_groups=mesh['wide'=8,'narrow'=4] {'wide'}, use_global_device_ids=true, to_apply=%region_25.26.clone | all-reduce | flops 2048 | bytes 8192
  934.5 88.3 %reduce-scatter.16.cloned.1.call-done = bf16[256,2048]{1,0:T(8,128)(2,1)} async-done(((bf16[2048,2048]{1,0:T(8,128)(2,1)}), bf16[256,2048]{1,0:T(8,128)(2,1)}) %reduce-scatter.16.cloned.1.call-update) | async-done | bytes 1048592 | tf_op jit(solution)/shard_map/reduce_scatter | solution.py:199
  1025.6 87.5 %reduce-scatter.18.cloned.1.call-done = bf16[2048,256]{1,0:T(8,128)(2,1)} async-done(((bf16[2048,2048]{1,0:T(8,128)(2,1)}), bf16[2048,256]{1,0:T(8,128)(2,1)}) %reduce-scatter.18.cloned.1.call-update) | async-done | bytes 1048592 | tf_op jit(solution)/shard_map/reduce_scatter | solution.py:205
  1115.8 11.6 add_convert_fusion.1
  1127.3 12.2 add_convert_fusion
  1145.3 30.6 %reduce-scatter.22.cloned.1.call-done = bf16[256,3]{1,0:T(8,128)(2,1)} async-done(((bf16[2048,3]{1,0:T(8,128)(2,1)}), bf16[256,3]{1,0:T(8,128)(2,1)}) %reduce-scatter.22.cloned.1.call-update) | async-done | bytes 1552
  1177.4 68.7 %reduce-scatter.12.cloned.1.call-done = bf16[3,256,512]{1,2,0:T(8,128)(2,1)} async-done(((bf16[3,2048,512]{1,2,0:T(8,128)(2,1)}), bf16[3,256,512]{1,2,0:T(8,128)(2,1)}) %reduce-scatter.12.cloned.1.call-update) | async-done | bytes 786448 | tf_op jit(solution)/shard_map/reduce_scatter | solution.py:193
  1248.7 127.4 %reduce-scatter.20.cloned.1.call-done = bf16[256,6,512]{2,0,1:T(8,128)(2,1)} async-done(((bf16[2048,6,512]{2,0,1:T(8,128)(2,1)}), bf16[256,6,512]{2,0,1:T(8,128)(2,1)}) %reduce-scatter.20.cloned.1.call-update) | async-done | bytes 1572880 | tf_op jit(solution)/shard_map/reduce_scatter | solution.py:208
  (296 shorter events, 259.7 us)
Async XLA Ops:
  7.2 95.0 %copy-start = (bf16[512,2048]{1,0:T(8,128)(2,1)S(1)}, bf16[512,2048]{1,0:T(8,128)(2,1)}, u32[]{:S(2)}) copy-start(bf16[512,2048]{1,0:T(8,128)(2,1)} %param.26) | copy-start | bytes 6291460
  7.2 274.9 %all-reduce.7.cloned.1.call-start = ((), (), s32[]{:S(2)}) async-start(), calls=%async_computation.7 | async-start | bytes 16777216 | tf_op jit(solution)/shard_map/psum | solution.py:105
  10.2 49.9 %copy-start.37 = (f32[1024]{0:T(1024)}, f32[1024]{0:T(1024)S(1)}, u32[]{:S(2)}) copy-start(f32[1024]{0:T(1024)S(1)} %broadcast_multiply_fusion.5) | copy-start | bytes 12292
  13.7 46.5 %copy-start.39 = (f32[1024]{0:T(1024)}, f32[1024]{0:T(1024)S(1)}, u32[]{:S(2)}) copy-start(f32[1024]{0:T(1024)S(1)} %add_rsqrt_fusion.1) | copy-start | bytes 12292
  13.7 17.1 %copy-start.33 = (f32[16,2048]{1,0:T(8,128)S(1)}, f32[16,2048]{1,0:T(8,128)}, u32[]{:S(2)}) copy-start(f32[16,2048]{1,0:T(8,128)} %param.20) | copy-start | bytes 393220
  13.7 17.1 %copy-start.45 = (f32[3,2048]{1,0:T(4,128)S(1)}, f32[3,2048]{1,0:T(4,128)}, u32[]{:S(2)}) copy-start(f32[3,2048]{1,0:T(4,128)} %param.24) | copy-start | bytes 73732
  30.8 25.4 %copy-start.41 = (s32[1,16]{1,0:T(1,128)S(1)}, s32[1,16]{1,0:T(1,128)}, u32[]{:S(2)}) copy-start(s32[1,16]{1,0:T(1,128)} %param.21) | copy-start | bytes 196
  30.8 25.4 %copy-start.54 = (s32[1,16]{1,0:T(1,128)S(1)}, s32[1,16]{1,0:T(1,128)}, u32[]{:S(2)}) copy-start(s32[1,16]{1,0:T(1,128)} %param.22) | copy-start | bytes 196
  39.8 20.4 %copy-start.7 = (bf16[1024,2048]{1,0:T(8,128)(2,1)S(1)}, bf16[1024,2048]{1,0:T(8,128)(2,1)}, u32[]{:S(2)}) copy-start(bf16[1024,2048]{1,0:T(8,128)(2,1)} %param.18) | copy-start | bytes 12582916
  56.3 243.9 %copy-start.43 = (s32[16]{0:T(128)}, s32[16]{0:T(128)S(1)}, u32[]{:S(2)}) copy-start(s32[16]{0:T(128)S(1)} %add_bitcast_fusion) | copy-start | bytes 196
  109.5 437.7 %all-reduce.9.cloned.1.call-start = ((), (), s32[]{:S(2)}) async-start(), calls=%async_computation.8 | async-start | bytes 16777216 | tf_op jit(solution)/shard_map/psum | solution.py:122
  308.1 31.0 %copy-start.19 = (bf16[1024,2048]{1,0:T(8,128)(2,1)}, bf16[1024,2048]{1,0:T(8,128)(2,1)S(1)}, u32[]{:S(2)}) copy-start(bf16[1024,2048]{1,0:T(8,128)(2,1)S(1)} %add_convert_fusion.2) | copy-start | bytes 12582916
  374.3 434.0 %all-reduce.13.cloned.1.call-start = ((), (), s32[]{:S(2)}) async-start(), calls=%async_computation.17 | async-start | bytes 16777216 | tf_op jit(solution)/shard_map/psum | solution.py:111
  634.8 259.0 %all-reduce.11.cloned.1.call-start = ((), (), s32[]{:S(2)}) async-start(), calls=%async_computation.9 | async-start | bytes 131072 | tf_op jit(solution)/shard_map/psum | solution.py:179
  641.8 169.9 %copy-start.38 = (f32[1024]{0:T(1024)S(1)}, f32[1024]{0:T(1024)}, u32[]{:S(2)}) copy-start(f32[1024]{0:T(1024)} %copy-done.37) | copy-start | bytes 12292
  641.8 169.9 %copy-start.40 = (f32[1024]{0:T(1024)S(1)}, f32[1024]{0:T(1024)}, u32[]{:S(2)}) copy-start(f32[1024]{0:T(1024)} %copy-done.39) | copy-start | bytes 12292
  851.5 81.3 %reduce-scatter.14.cloned.1.call-start = ((), (), s32[]{:S(2)}) async-start(), calls=%async_computation.11 | async-start | bytes 2359296 | tf_op jit(solution)/shard_map/reduce_scatter | solution.py:196
  857.5 165.3 %reduce-scatter.16.cloned.1.call-start = ((), (), s32[]{:S(2)}) async-start(), calls=%async_computation.12 | async-start | bytes 9437184 | tf_op jit(solution)/shard_map/reduce_scatter | solution.py:199
  871.8 241.3 %reduce-scatter.18.cloned.1.call-start = ((), (), s32[]{:S(2)}) async-start(), calls=%async_computation.13 | async-start | bytes 9437184 | tf_op jit(solution)/shard_map/reduce_scatter | solution.py:205
  887.2 256.6 %reduce-scatter.24.cloned.1.call-start = ((), (), s32[]{:S(2)}) async-start(), calls=%async_computation.16 | async-start | bytes 147456
  888.1 287.8 %reduce-scatter.22.cloned.1.call-start = ((), (), s32[]{:S(2)}) async-start(), calls=%async_computation.15 | async-start | bytes 589824
  896.1 350.0 %reduce-scatter.12.cloned.1.call-start = ((), (), s32[]{:S(2)}) async-start(), calls=%async_computation.10 | async-start | bytes 7077888 | tf_op jit(solution)/shard_map/reduce_scatter | solution.py:193
  907.6 468.5 %reduce-scatter.20.cloned.1.call-start = ((), (), s32[]{:S(2)}) async-start(), calls=%async_computation.14 | async-start | bytes 14155776 | tf_op jit(solution)/shard_map/reduce_scatter | solution.py:208
  1127.3 252.2 %copy-start.1 = (bf16[512,2048]{1,0:T(8,128)(2,1)S(1)}, bf16[512,2048]{1,0:T(8,128)(2,1)}, u32[]{:S(2)}) copy-start(bf16[512,2048]{1,0:T(8,128)(2,1)} %param.26) | copy-start | bytes 6291460
  (65 other events, 362.2 us)
Sparse Core Ops, SparseCore 0:
  109.6 172.4 all-reduce.6
  374.4 172.7 all-reduce.8
  635.0 173.3 all-reduce.12
  851.6 42.1 all-reduce.10
  896.5 35.7 reduce-scatter.13
  934.5 88.2 reduce-scatter.15
  1025.1 87.9 reduce-scatter.17
  1115.3 28.5 reduce-scatter.23
  1146.8 29.0 reduce-scatter.21
  1178.0 68.0 reduce-scatter.11
  1248.4 127.5 reduce-scatter.19
where the time goes:
time: 1390 us
  waiting for transfers between devices  898 us (65%)
  matrix products  257 us (18%)
  other arithmetic  126 us (9%)
  local copies, waits for them, and re-layouts  56.8 us (4%)
  blocking collectives  31.3 us (2%)
  between operations  15.7 us (1%)
    psum x1, waiting for transfers between devices, body(): lax.psum(jnp.dot(hidden, w_down, preferred_element_type=f32).astype(jnp.b...  167 us
    psum x1, waiting for transfers between devices, body(): lax.psum(jnp.dot(heads_out, w_out, preferred_element_type=f32), 'narrow')  160 us
    psum x1, waiting for transfers between devices, body(): lax.psum(jnp.dot(d_pre, w_up.T, preferred_element_type=f32), 'narrow')  159 us
    reduce_scatter x1, waiting for transfers between devices, body(): lax.psum_scatter(grad_w_mod.astype(jnp.bfloat16), 'wide', scatter_dimensi...  127 us
    reduce_scatter x1, waiting for transfers between devices, body(): lax.psum_scatter(grad_w_up.astype(jnp.bfloat16), 'wide', scatter_dimensio...  88.3 us
    reduce_scatter x1, waiting for transfers between devices, body(): lax.psum_scatter(grad_w_down.astype(jnp.bfloat16), 'wide', scatter_dimens...  87.5 us
    reduce_scatter x1, waiting for transfers between devices, body(): lax.psum_scatter(grad_w_qkv.astype(jnp.bfloat16), 'wide', scatter_dimensi...  68.7 us
    dot_general x6, matrix products, per_token(): return jnp.dot(member, mod_full[:, column], precision=highest)  39.6 us
  transfers between devices with their start and end apart: 11, of which 10 were waited for; matrix products, arithmetic and copies ran while one was open for 9% of the time, Pallas kernels for 0%

commit v1 on v0

--- a/solution.py
+++ b/solution.py
@@ -108,8 +108,11 @@
     mixed_b = (normed_b * (1.0 + scale_b) + shift_b).astype(half)
     hidden_pre = jnp.dot(mixed_b, w_up, preferred_element_type=f32) + b_up
     hidden = jax.nn.gelu(hidden_pre, approximate=False).astype(half)
-    mlp_out = lax.psum(
-        jnp.dot(hidden, w_down, preferred_element_type=f32).astype(jnp.bfloat16), "narrow"
+    mlp_out = jnp.sum(
+        lax.all_gather(
+            jnp.dot(hidden, w_down, preferred_element_type=f32).astype(jnp.bfloat16), "narrow"
+        ),
+        axis=0,
     ).astype(jnp.float32)
     result = (middle + gate_b * mlp_out).astype(half)
     grad_out = cotangent.astype(f32)

time: 1390 us -> 1520 us (1.094)
  waiting for transfers between devices: 898 us -> 1010 us
    all_gather x0 -> x1, waiting for transfers between devices: none -> 158 us  [body(): lax.all_gather(jnp.dot(hidden, w_down, preferred_element_type=f32).astype...]
    psum x1, waiting for transfers between devices: 167 us -> 91.4 us  [body(): lax.psum(jnp.einsum('tiv,idv->td', d_proj, w_qkv, preferred_element_type=...]
    psum x1, waiting for transfers between devices: 5.66 us -> 34.7 us  [body(): lax.psum(jnp.dot(flat_modes, w_mod.reshape(width, 6 * local_width).T, pre...]
    unnamed x13 -> x14, waiting for transfers between devices: 35.1 us -> 16.4 us
    unnamed x113 -> x119, local copies, waits for them, and re-layouts: 33.3 us -> 35.4 us
  transfers between devices with their start and end apart: 11 -> 12, of which waited for: 10 -> 10; matrix products, arithmetic and copies ran while one was open for 9% -> 7% of each run, Pallas kernels for 0% -> 0%
where the time goes in v1:
time: 1520 us; the launch traced here: 1510 us
  waiting for transfers between devices  1010 us (66%)
  matrix products  257 us (17%)
  other arithmetic  133 us (9%)
  local copies, waits for them, and re-layouts  59 us (4%)
  blocking collectives  31.3 us (2%)
  between operations  15.8 us (1%)
    psum x1, waiting for transfers between devices, body(): lax.psum(jnp.dot(d_pre, w_up.T, preferred_element_type=f32), 'narrow')  172 us
    psum x1, waiting for transfers between devices, body(): lax.psum(jnp.dot(heads_out, w_out, preferred_element_type=f32), 'narrow')  166 us
    all_gather x1, waiting for transfers between devices, body(): lax.all_gather(jnp.dot(hidden, w_down, preferred_element_type=f32).astype...  158 us
    reduce_scatter x1, waiting for transfers between devices, body(): lax.psum_scatter(grad_w_mod.astype(jnp.bfloat16), 'wide', scatter_dimensi...  127 us
    psum x1, waiting for transfers between devices, body(): lax.psum(jnp.einsum('tiv,idv->td', d_proj, w_qkv, preferred_element_type=...  91.4 us
    reduce_scatter x1, waiting for transfers between devices, body(): lax.psum_scatter(grad_w_up.astype(jnp.bfloat16), 'wide', scatter_dimensio...  88.6 us
    reduce_scatter x1, waiting for transfers between devices, body(): lax.psum_scatter(grad_w_down.astype(jnp.bfloat16), 'wide', scatter_dimens...  87.4 us
    reduce_scatter x1, waiting for transfers between devices, body(): lax.psum_scatter(grad_w_qkv.astype(jnp.bfloat16), 'wide', scatter_dimensi...  67.8 us
  transfers between devices with their start and end apart: 12, of which 10 were waited for; matrix products, arithmetic and copies ran while one was open for 7% of the time, Pallas kernels for 0%

profile of v1, /device:TPU:0, one launch (start us, length us, event | category | flops | bytes accessed | tf_op | source)
XLA Modules:
  0.0 1507.8 jit_solution(1222937744132881150)
XLA Ops:
  13.7 17.1 %copy.59 = bf16[2048,6,512]{0,2,1:T(8,128)(2,1)} copy(bf16[2048,6,512]{2,0,1:T(8,128)(2,1)} %param.30) | data formatting | bytes 25165824 | tf_op args[12]
  39.8 15.2 %all_gather.9 = f32[16,6,2048]{2,1,0:T(8,128)S(1)} all-gather(f32[16,6,512]{2,1,0:T(8,128)S(1)} %reshape.223), channel_id=1, replica_groups=mesh['wide'=8,'narrow'=4] {'narrow'}, dimensions={2}, use_global_device_ids=true | all-gather | bytes 983040 | tf_op jit(solution)/shard_map/all_gather | solution.py:60
  83.2 19.1 %while.27 = (s32[]{:T(128)}, bf16[2,512,4,128]{3,2,1,0:T(4,128)(2,1)}, f32[2,4,512]{2,1,0:T(4,128)}, f32[2,512]{1,0:T(2,128)S(1)}, f32[1024]{0:T(1024)S(1)}, /*i...) while((s32[]{:T(128)}, ...), condition=%wide.region_5.6_spmd, body=%wide.region_2.5_spmd.sunk | while | flops 1093400576 | bytes 44247296 | solution.py:103
  115.7 166.4 %all-reduce.6.cloned.1.call-done = f32[1024,2048]{1,0:T(8,128)} async-done(((f32[1024,2048]{1,0:T(8,128)}), f32[1024,2048]{1,0:T(8,128)}) %all-reduce.6.cloned.1.call-update) | async-done | bytes 8388624 | tf_op jit(solution)/shard_map/psum | solution.py:105
  308.2 31.2 %fusion.32 = (bf16[1024,2048]{1,0:T(8,128)(2,1)S(1)}, f32[1024,2048]{1,0:T(8,128)}) fusion(f32[2048]{0:T(1024)S(1)} %copy-done.53, bf16[1024,2048]{1,0:T(8,128)(2,1)S(1)} %add_convert_fusion.2, bf16[2048,2048]{1,0:T(8,128)(2,1)} %param.27), kind=kOutput, calls=%fused_computation.52 | convolution fusion | flops 8728346624 | bytes 25174016 | tf_op jit(solution)/shard_map/dot_general | solution.py:109
  351.8 158.2 %all-gather.3.cloned.1.call-done = bf16[4096,2048]{1,0:T(8,128)(2,1)} async-done(((bf16[1024,2048]{1,0:T(8,128)(2,1)}), bf16[4096,2048]{1,0:T(8,128)(2,1)}) %all-gather.3.cloned.1.call-update) | async-done | bytes 16777232 | tf_op jit(solution)/shard_map/all_gather | solution.py:112
  510.0 12.6 reduce_sum.130
  532.6 20.4 %fusion.117 = (bf16[2048]{0:T(1024)(128)(2,1)}, bf16[1024,2048]{1,0:T(8,128)(2,1)}) fusion(f32[1024,2048]{1,0:T(8,128)} %get-tuple-element.303, f32[2048]{0:T(1024)S(1)} %copy-done.53, bf16[2048,2048]{1,0:T(8,128)(2,1)} %param.29, f32[1024,2048]{1,0:T(8,128)} %get-tuple-element.305, bf16[1024,2048]{1,0:T(8,128)(2,1)} %param.19), kind=kOutput, calls=%fused_computation.182 | convolution fusion | flops 8625584128 | bytes 33566720 | tf_op jit(solution)/shard_map/dot_general | solution.py:120
  553.0 14.5 fusion.119
  567.6 172.2 %all-reduce.8.cloned.1.call-done = f32[1024,2048]{1,0:T(8,128)} async-done(((f32[1024,2048]{1,0:T(8,128)}), f32[1024,2048]{1,0:T(8,128)}) %all-reduce.8.cloned.1.call-update) | async-done | bytes 8388624 | tf_op jit(solution)/shard_map/psum | solution.py:125
  749.5 18.6 %multiply_convert_fusion.1 = (bf16[1024,2048]{1,0:T(8,128)(2,1)}, f32[1024,2048]{1,0:T(8,128)}) fusion(f32[1024,2048]{1,0:T(8,128)} %get-tuple-element.301, f32[1024]{0:T(1024)S(1)} %get-tuple-element.310, f32[1024]{0:T(1024)S(1)} %get-tuple-element.311, f32[1024,2048]{1,0:T(8,128)} %all-reduce.8.cloned.1.call-done, f32[1024,2048]{1,0:T(8,128)} %fusion.81, ...), kind=kLoop, calls=%fused_computation.62 | loop fusion | flops 25165824 | bytes 50348032 | tf_op jit(solution)/shard_map/convert_element_type | solution.py:127
  775.9 32.9 %while.28 = (s32[]{:T(128)}, f32[1024,4,128]{0,2,1:T(8,128)}, f32[1024,4,128]{0,2,1:T(8,128)}, f32[2,512,4,128]{3,1,2,0:T(8,128)}, bf16[2,512,4,128]{3,1,2,0:T(8...) while((s32[]{:T(128)}, f32[1024,4,128]{0,2,1:T(8,128)}, ...), condition=%wide.region_15.16_spmd.clone, body=%wide.region_13.15_spmd.clone.sunk | while | flops 2712139776 | bytes 139528592 | solution.py:149
  840.5 91.4 %all-reduce.10.cloned.1.call-done = bf16[1024,2048]{1,0:T(8,128)(2,1)} async-done(((bf16[1024,2048]{1,0:T(8,128)(2,1)}), bf16[1024,2048]{1,0:T(8,128)(2,1)}) %all-reduce.10.cloned.1.call-update) | async-done | bytes 4194320 | tf_op jit(solution)/shard_map/psum | solution.py:157
  980.2 34.7 %all-reduce.12.cloned.1.call-done = bf16[16,2048]{1,0:T(8,128)(2,1)} async-done(((bf16[16,2048]{1,0:T(8,128)(2,1)}), bf16[16,2048]{1,0:T(8,128)(2,1)}) %all-reduce.12.cloned.1.call-update) | async-done | bytes 65552 | tf_op jit(solution)/shard_map/psum | solution.py:182
  1017.3 14.2 convolution_convert_fusion.1
  1031.6 15.4 %convolution_convert_fusion = bf16[2048,2048]{1,0:T(8,128)(2,1)} fusion(bf16[1024,2048]{1,0:T(8,128)(2,1)} %copy-done.56, f32[1024,2048]{1,0:T(8,128)} %get-tuple-element.305, bf16[1024,2048]{1,0:T(8,128)(2,1)} %param.19), kind=kOutput, calls=%fused_computation.88 | convolution fusion | flops 8600420352 | bytes 25165824 | tf_op jit(solution)/shard_map/dot_general | solution.py:123
  1048.6 11.2 convert_bitcast_fusion
  1068.3 16.0 %all-reduce = bf16[2048]{0:T(1024)(128)(2,1)S(1)} all-reduce(bf16[2048]{0:T(1024)(128)(2,1)S(1)} %copy-done.47), channel_id=7, replica_groups=mesh['wide'=8,'narrow'=4] {'wide'}, use_global_device_ids=true, to_apply=%region_25.26.clone | all-reduce | flops 2048 | bytes 8192
  1086.8 12.2 add_convert_fusion
  1100.4 16.2 %reduce-scatter.22.cloned.1.call-done = bf16[256,3]{1,0:T(8,128)(2,1)} async-done(((bf16[2048,3]{1,0:T(8,128)(2,1)}), bf16[256,3]{1,0:T(8,128)(2,1)}) %reduce-scatter.22.cloned.1.call-update) | async-done | bytes 1552
  1118.2 88.6 %reduce-scatter.16.cloned.1.call-done = bf16[256,2048]{1,0:T(8,128)(2,1)} async-done(((bf16[2048,2048]{1,0:T(8,128)(2,1)}), bf16[256,2048]{1,0:T(8,128)(2,1)}) %reduce-scatter.16.cloned.1.call-update) | async-done | bytes 1048592 | tf_op jit(solution)/shard_map/reduce_scatter | solution.py:202
  1209.6 87.4 %reduce-scatter.18.cloned.1.call-done = bf16[2048,256]{1,0:T(8,128)(2,1)} async-done(((bf16[2048,2048]{1,0:T(8,128)(2,1)}), bf16[2048,256]{1,0:T(8,128)(2,1)}) %reduce-scatter.18.cloned.1.call-update) | async-done | bytes 1048592 | tf_op jit(solution)/shard_map/reduce_scatter | solution.py:208
  1299.6 67.8 %reduce-scatter.12.cloned.1.call-done = bf16[3,256,512]{1,2,0:T(8,128)(2,1)} async-done(((bf16[3,2048,512]{1,2,0:T(8,128)(2,1)}), bf16[3,256,512]{1,2,0:T(8,128)(2,1)}) %reduce-scatter.12.cloned.1.call-update) | async-done | bytes 786448 | tf_op jit(solution)/shard_map/reduce_scatter | solution.py:196
  1370.0 127.2 %reduce-scatter.20.cloned.1.call-done = bf16[256,6,512]{2,0,1:T(8,128)(2,1)} async-done(((bf16[2048,6,512]{2,0,1:T(8,128)(2,1)}), bf16[256,6,512]{2,0,1:T(8,128)(2,1)}) %reduce-scatter.20.cloned.1.call-update) | async-done | bytes 1572880 | tf_op jit(solution)/shard_map/reduce_scatter | solution.py:211
  (306 shorter events, 282.4 us)
Async XLA Ops:
  7.2 95.1 %copy-start = (bf16[512,2048]{1,0:T(8,128)(2,1)S(1)}, bf16[512,2048]{1,0:T(8,128)(2,1)}, u32[]{:S(2)}) copy-start(bf16[512,2048]{1,0:T(8,128)(2,1)} %param.26) | copy-start | bytes 6291460
  7.2 274.9 %all-reduce.6.cloned.1.call-start = ((), (), s32[]{:S(2)}) async-start(), calls=%async_computation.7 | async-start | bytes 16777216 | tf_op jit(solution)/shard_map/psum | solution.py:105
  10.2 49.9 %copy-start.37 = (f32[1024]{0:T(1024)}, f32[1024]{0:T(1024)S(1)}, u32[]{:S(2)}) copy-start(f32[1024]{0:T(1024)S(1)} %broadcast_multiply_fusion.5) | copy-start | bytes 12292
  13.7 46.5 %copy-start.39 = (f32[1024]{0:T(1024)}, f32[1024]{0:T(1024)S(1)}, u32[]{:S(2)}) copy-start(f32[1024]{0:T(1024)S(1)} %add_rsqrt_fusion.1) | copy-start | bytes 12292
  56.2 466.4 %copy-start.43 = (s32[16]{0:T(128)}, s32[16]{0:T(128)S(1)}, u32[]{:S(2)}) copy-start(s32[16]{0:T(128)S(1)} %add_bitcast_fusion) | copy-start | bytes 196
  109.6 400.4 %all-gather.3.cloned.1.call-start = ((), (), s32[]{:S(2)}) async-start(), calls=%async_computation.16 | async-start | bytes 20971520 | tf_op jit(solution)/shard_map/all_gather | solution.py:112
  301.1 40.3 %slice-start.7 = ((s8[8388608]{0:T(1024)(128)(4,1)}), s8[4194304]{0:T(1024)(128)(4,1)S(1)}, s32[]{:S(2)}) async-start(s8[8388608]{0:T(1024)(128)(4,1)} %bitcast.251), calls=%async_computation.26 | async-start | bytes 8388608
  308.2 31.2 %copy-start.18 = (bf16[1024,2048]{1,0:T(8,128)(2,1)}, bf16[1024,2048]{1,0:T(8,128)(2,1)S(1)}, u32[]{:S(2)}) copy-start(bf16[1024,2048]{1,0:T(8,128)(2,1)S(1)} %add_convert_fusion.2) | copy-start | bytes 12582916
  308.2 33.2 %slice-start.8 = ((s8[8388608]{0:T(1024)(128)(4,1)}), s8[4194304]{0:T(1024)(128)(4,1)S(1)}, s32[]{:S(2)}) async-start(s8[8388608]{0:T(1024)(128)(4,1)} %bitcast.251), calls=%async_computation.27 | async-start | bytes 8388608
  351.7 388.1 %all-reduce.8.cloned.1.call-start = ((), (), s32[]{:S(2)}) async-start(), calls=%async_computation.8 | async-start | bytes 16777216 | tf_op jit(solution)/shard_map/psum | solution.py:125
  567.5 364.4 %all-reduce.10.cloned.1.call-start = ((), (), s32[]{:S(2)}) async-start(), calls=%async_computation.9 | async-start | bytes 8388608 | tf_op jit(solution)/shard_map/psum | solution.py:157
  827.2 187.7 %all-reduce.12.cloned.1.call-start = ((), (), s32[]{:S(2)}) async-start(), calls=%async_computation.10 | async-start | bytes 131072 | tf_op jit(solution)/shard_map/psum | solution.py:182
  840.5 96.4 %copy-start.38 = (f32[1024]{0:T(1024)S(1)}, f32[1024]{0:T(1024)}, u32[]{:S(2)}) copy-start(f32[1024]{0:T(1024)} %copy-done.37) | copy-start | bytes 12292
  840.5 96.4 %copy-start.40 = (f32[1024]{0:T(1024)S(1)}, f32[1024]{0:T(1024)}, u32[]{:S(2)}) copy-start(f32[1024]{0:T(1024)} %copy-done.39) | copy-start | bytes 12292
  973.3 41.7 %copy-start.20 = (f32[16,2048]{1,0:T(8,128)S(1)}, f32[16,2048]{1,0:T(8,128)}, u32[]{:S(2)}) copy-start(f32[16,2048]{1,0:T(8,128)} %copy-done.19) | copy-start | bytes 393220
  973.3 42.6 %copy-start.49 = (s32[1,16]{1,0:T(1,128)S(1)}, s32[1,16]{1,0:T(1,128)}, u32[]{:S(2)}) copy-start(s32[1,16]{1,0:T(1,128)} %param.23) | copy-start | bytes 196
  973.3 111.7 %reduce-scatter.14.cloned.1.call-start = ((), (), s32[]{:S(2)}) async-start(), calls=%async_computation.12 | async-start | bytes 2359296 | tf_op jit(solution)/shard_map/reduce_scatter | solution.py:199
  979.3 119.7 %reduce-scatter.24.cloned.1.call-start = ((), (), s32[]{:S(2)}) async-start(), calls=%async_computation.18 | async-start | bytes 147456
  980.2 136.5 %reduce-scatter.22.cloned.1.call-start = ((), (), s32[]{:S(2)}) async-start(), calls=%async_computation.17 | async-start | bytes 589824
  1017.3 189.5 %reduce-scatter.16.cloned.1.call-start = ((), (), s32[]{:S(2)}) async-start(), calls=%async_computation.13 | async-start | bytes 9437184 | tf_op jit(solution)/shard_map/reduce_scatter | solution.py:202
  1031.6 265.4 %reduce-scatter.18.cloned.1.call-start = ((), (), s32[]{:S(2)}) async-start(), calls=%async_computation.14 | async-start | bytes 9437184 | tf_op jit(solution)/shard_map/reduce_scatter | solution.py:208
  1047.1 320.4 %reduce-scatter.12.cloned.1.call-start = ((), (), s32[]{:S(2)}) async-start(), calls=%async_computation.11 | async-start | bytes 7077888 | tf_op jit(solution)/shard_map/reduce_scatter | solution.py:196
  1059.9 437.3 %reduce-scatter.20.cloned.1.call-start = ((), (), s32[]{:S(2)}) async-start(), calls=%async_computation.15 | async-start | bytes 14155776 | tf_op jit(solution)/shard_map/reduce_scatter | solution.py:211
  1086.8 413.9 %copy-start.1 = (bf16[512,2048]{1,0:T(8,128)(2,1)S(1)}, bf16[512,2048]{1,0:T(8,128)(2,1)}, u32[]{:S(2)}) copy-start(bf16[512,2048]{1,0:T(8,128)(2,1)} %param.26) | copy-start | bytes 6291460
  (69 other events, 468.2 us)
Sparse Core Ops, SparseCore 0:
  109.7 172.3 all-reduce.5
  351.9 158.0 all-gather.2
  567.6 172.1 all-reduce.7
  827.4 104.5 all-reduce.9
  973.4 41.4 all-reduce.11
  1017.7 35.7 reduce-scatter.13
  1055.7 28.8 reduce-scatter.23
  1087.5 29.0 reduce-scatter.21
  1118.9 87.8 reduce-scatter.15
  1208.9 87.9 reduce-scatter.17
  1299.3 68.1 reduce-scatter.11
  1369.6 127.5 reduce-scatter.19
